TPU v7x, 512 devices: a whole 4x8x8 slice. The times are simulated.
512 devices in a mesh: tensor: 16 (over x_lo, y), adapter: 32 (over x_hi, z, core).
Axes of the slice: x: 4 (x_hi: 2, x_lo: 2; x = x_hi * 2 + x_lo), y: 8, z: 8, core: 2. Of those that a mesh axis runs over, the one named last changes fastest.
Arguments:
- tokens: bfloat16 [65536, 8192], P(('tensor', 'adapter')), may hold values from -6 to 6
- base_key_weight: bfloat16 [8192, 768], P(None, 'tensor'), may hold values from -0.0625 to 0.0625
- adapter_down_factors: bfloat16 [32, 8192, 64], P('adapter'), may hold values from -0.0625 to 0.0625
- adapter_up_factors: bfloat16 [32, 64, 768], P('adapter'), may hold values from -0.75 to 0.75
- token_adapter_index: int32 [65536, 1], P(('tensor', 'adapter')), may hold values from 0 to 31; in each aligned block of 128 rows (0 to 127, 128 to 255, ...) at most 8 rows name the same one
- placement: int32 [32], replicated, may hold values from 0 to 31, each once
Outputs:
- keys_out: bfloat16 [65536, 768], P(('tensor', 'adapter'))
Inputs may be any that keep to these rules, and one draw needn't show every extreme that they name: `token_adapter_index`: in each aligned block of 128 tokens (the tokens of one device) no adapter is named by more than 8 tokens, a bound that some block reaches. `placement`: each slot holds exactly one adapter.
All inputs are finite; a program needn't handle non-finite values.
Results may differ from a plain program's by a relative error of at most 0.005.
Values may be sent and summed in bfloat16 or wider, within the bound.
No kernel may reach another device: no remote copies, remote signals or barrier semaphores. Data moves between devices by JAX's collectives and lax.ppermute only.
A program may use at most 64 MiB of HBM per device.

v0:
```python
import functools

import jax
import jax.numpy as jnp
from jax import lax
from jax.experimental import pallas as pl
from jax.experimental.pallas import tpu as pltpu
from jax.sharding import Mesh, PartitionSpec as P


AXES = ("xl", "y", "xh", "z", "c")
SIZES = (2, 8, 2, 8, 2)
XRING = ("xh", "xl")
LANES = 128
f32 = jnp.float32
bf16 = jnp.bfloat16
i32 = jnp.int32
VMEM = pl.BlockSpec(memory_space=pltpu.VMEM)
SMEM = pl.BlockSpec(memory_space=pltpu.SMEM)


def pairs_of(move):
    out = []
    for flat in range(512):
        rest, at = flat, []
        for size in reversed(SIZES):
            at.append(rest % size)
            rest //= size
        to = move(*reversed(at))
        index = 0
        for size, place in zip(SIZES, to):
            index = index * size + place % size
        out.append((flat, index))
    return out


def shift(value, axis, by):
    n = lax.axis_size(axis)
    return lax.ppermute(value, axis, [(i, (i + by) % n) for i in range(n)])


def exchange(value, axes):
    return lax.all_to_all(value, axes, split_axis=0, concat_axis=0, tiled=True)


def nt(a, b):
    return lax.dot_general(a, b, (((1,), (1,)), ((), ())), preferred_element_type=f32)


def params(mib):
    return pltpu.CompilerParams(vmem_limit_bytes=mib << 20)


def cost(flops, moved):
    return pl.CostEstimate(flops=int(flops), bytes_accessed=int(moved), transcendentals=0)


def pack_kernel(tok, ids, out):
    part = tok.shape[1]
    out[0, :, :part] = tok[...]
    out[0, :, part:] = jnp.broadcast_to(ids[0:1, :], (out.shape[1], LANES))


def pack(tokens, ids):
    rows, width = tokens.shape
    part = width // 4
    return pl.pallas_call(
        pack_kernel,
        grid=(4,),
        in_specs=[
            pl.BlockSpec((rows, part), lambda i: (0, i)),
            pl.BlockSpec((8, LANES), lambda i: (0, 0)),
        ],
        out_specs=pl.BlockSpec((1, rows, part + LANES), lambda i: (i, 0, 0)),
        out_shape=jax.ShapeDtypeStruct((4, rows, part + LANES), bf16),
        cost_estimate=cost(0, 4 * tokens.size),
        compiler_params=params(8),
        name="pack_tokens",
    )(tokens, ids)


HELD = [(0, 0, 0), (1, 0, 0)]
HELD += [(side, step, flip) for step in (1, 2, 3) for side in (0, 1) for flip in (0, 1)]
HELD += [(0, 4, 0), (1, 4, 0)]


def slot_of(place, entry, core):
    side, step, flip = entry
    xh, z = place[2], place[3]
    line = jnp.bitwise_and(z + step * (2 * core - 1) + 8, 7)
    return (16 * (1 - xh if side else xh) + 2 * line + (1 - core if flip else core)).astype(f32)


def factors_kernel(place, down, up, own, away):
    part = own.shape[1] - up.shape[1]
    for at, out in ((place[0], own), (3 - place[0], away)):
        out[:, :part] = down[:, pl.ds(pl.multiple_of(at * part, LANES), part)]
        out[:, part:] = up[...]


def factors(place, down, up):
    rank, width = down.shape
    piece = jax.ShapeDtypeStruct((rank, width // 4 + up.shape[1]), bf16)
    return pl.pallas_call(
        factors_kernel,
        in_specs=[SMEM, VMEM, VMEM],
        out_specs=[VMEM] * 2,
        out_shape=[piece] * 2,
        cost_estimate=cost(0, 4 * down.size),
        compiler_params=params(6),
        name="factors",
    )(place, down, up)


def panels_kernel(place, panel, out):
    wide, part = out.shape[1:]
    for d in range(2):
        at = pl.multiple_of((2 * place[2] + d) * part, LANES)
        both = panel[:, pl.ds(at, part)]
        rows = jnp.where(place[4] == 0, both[:wide], both[wide:])
        for y in range(8):
            out[8 * d + y] = rows


def spread_panels(place, panel):
    wide, part = panel.shape[0] // 2, panel.shape[1] // 4
    return pl.pallas_call(
        panels_kernel,
        in_specs=[SMEM, VMEM],
        out_specs=VMEM,
        out_shape=jax.ShapeDtypeStruct((16, wide, part), bf16),
        cost_estimate=cost(0, 40 * wide * part),
        compiler_params=params(6),
        name="spread_panels",
    )(place, panel)


def head_kernel(ref, out):
    out[...] = ref[0:out.shape[0], :]


def head(value, rows):
    return pl.pallas_call(
        head_kernel,
        in_specs=[VMEM],
        out_specs=VMEM,
        out_shape=jax.ShapeDtypeStruct((rows, value.shape[1]), value.dtype),
        cost_estimate=cost(0, 4 * rows * value.shape[1]),
        compiler_params=params(4),
        name="head",
    )(value)


def join_kernel(*refs):
    out, at = refs[-1], 0
    for ref in refs[:-1]:
        out[at:at + ref.shape[0], :] = ref[...]
        at += ref.shape[0]


def join(parts):
    rows = sum(p.shape[0] for p in parts)
    return pl.pallas_call(
        join_kernel,
        in_specs=[VMEM] * len(parts),
        out_specs=VMEM,
        out_shape=jax.ShapeDtypeStruct((rows, parts[0].shape[1]), parts[0].dtype),
        cost_estimate=cost(0, 4 * rows * parts[0].shape[1]),
        compiler_params=params(6),
        name="join",
    )(*parts)


def token_rows(ref):
    return ref[:, : ref.shape[1] - LANES]


def token_ids(ref):
    part = ref.shape[1] - LANES
    return jnp.concatenate([ref[s * LANES:s * LANES + 8, part:] for s in range(4)], axis=1)[0:1].astype(f32)


def base_kernel(place, base, mine, other, low, out):
    cols, rows = base.shape[0], out.shape[2]
    out[:, cols:, :] = low[...]
    for o, ref in enumerate((mine, other)):
        at = jnp.bitwise_xor(place[4], o)
        product = nt(base[...], token_rows(ref)).astype(bf16)
        for x in range(4):
            out[2 * x + at, :cols, :] = product[:, x * rows:(x + 1) * rows]


def base_product(place, base, mine, other, low):
    cols, part = base.shape
    toks = mine.shape[0]
    return pl.pallas_call(
        base_kernel,
        in_specs=[SMEM] + [VMEM] * 4,
        out_specs=VMEM,
        out_shape=jax.ShapeDtypeStruct((8, cols + low.shape[1], toks // 4), bf16),
        cost_estimate=cost(4 * cols * part * toks, 2 * (base.size + 2 * mine.size)),
        compiler_params=params(20),
        name="base_product",
    )(place, base, mine, other, low)


def low_kernel(rank, part, entries, last, place, *refs):
    count = len(refs) - 4 - last
    blocks, (mine, other) = refs[:count], refs[count:count + 2]
    new, ups = refs[-2:]
    w = jnp.concatenate([r[:, :part] for r in blocks], axis=0)
    at = 0
    for r in blocks:
        ups[at:at + r.shape[0], :] = r[:, part:]
        at += r.shape[0]
    for o, ref in enumerate((mine, other)):
        product = nt(w, token_rows(ref))
        ids = token_ids(ref)
        total = refs[count + 2][o] if last else jnp.zeros(new.shape[1:], f32)
        for a, entry in enumerate(entries):
            hit = ids == slot_of(place, entry, place[4])
            total = total + jnp.where(hit, product[a * rank:(a + 1) * rank], 0.0)
        if last:
            sent, rows = total.astype(bf16), new.shape[2]
            for x in range(4):
                new[2 * x + jnp.bitwise_xor(place[4], o)] = sent[:, x * rows:(x + 1) * rows]
        else:
            new[o] = total


def low_product(rank, part, entries, place, blocks, mine, other, old=None):
    rows = sum(b.shape[0] for b in blocks)
    toks = mine.shape[0]
    lanes = blocks[0].shape[1] - part
    last = old is not None
    if last:
        result = jax.ShapeDtypeStruct((8, rank, toks // 4), bf16)
    else:
        result = jax.ShapeDtypeStruct((2, rank, toks), f32)
    operands = (*blocks, mine, other) + ((old,) if last else ())
    return pl.pallas_call(
        functools.partial(low_kernel, rank, part, entries, last),
        in_specs=[SMEM] + [VMEM] * len(operands),
        out_specs=[VMEM] * 2,
        out_shape=[result, jax.ShapeDtypeStruct((rows, lanes), bf16)],
        cost_estimate=cost(4 * rows * part * toks, 2 * rows * part),
        compiler_params=params(20),
        name="low_product",
    )(place, *operands)


def final_kernel(rank, wide, place, got, u_mine0, u_mine1, u_other0, u_other1, ids, out):
    rows = got.shape[2]
    cols = got.shape[1] - rank
    base = []
    low = jnp.zeros((rank, rows), f32)
    for c in range(2):
        total = jnp.zeros((cols, rows), f32)
        for x in range(4):
            total = total + got[2 * x + c, :cols, :].astype(f32)
            low = low + got[2 * x + c, cols:, :].astype(f32)
        base.append(total)
    base = jnp.concatenate(
        [base[c][t * wide:(t + 1) * wide] for t in range(cols // wide) for c in range(2)], axis=0
    )
    low = low.astype(bf16).astype(f32)
    names = ids[0:1, :].astype(f32)
    delta = None
    for o, k, u in ((0, 0, u_mine0), (1, 0, u_other0), (0, 1, u_mine1), (1, 1, u_other1)):
        core = 1 - place[4] if o else place[4]
        entries = HELD[8 * k:8 * k + 8]
        spread = jnp.concatenate(
            [jnp.where(names == slot_of(place, entry, core), low, 0.0) for entry in entries], axis=0
        )
        term = jnp.dot(spread.T.astype(bf16), u[...], preferred_element_type=f32)
        delta = term if delta is None else delta + term
    out[...] = (base.T + delta.astype(bf16).astype(f32)).astype(bf16)


def finish(rank, wide, place, got, ups, ids):
    rows = got.shape[2]
    return pl.pallas_call(
        functools.partial(final_kernel, rank, wide),
        in_specs=[SMEM] + [VMEM] * 6,
        out_specs=VMEM,
        out_shape=jax.ShapeDtypeStruct((rows, 2 * (got.shape[1] - rank)), bf16),
        cost_estimate=cost(8 * ups[0].size * rows, 2 * got.size),
        compiler_params=params(20),
        name="finish",
    )(place, got, *ups, ids)


def on_device(tokens, base_key_weight, adapter_down_factors, adapter_up_factors, token_adapter_index, placement):
    rows, width = tokens.shape
    xl, xh, z, c = (lax.axis_index(a) for a in ("xl", "xh", "z", "c"))
    x = 2 * xh + xl
    part = width // 4
    table = placement.shape[0]
    rank = adapter_up_factors.shape[1]
    columns = jnp.arange(table, dtype=i32)
    place = jnp.stack([x, 1 - 2 * c, xh, z, c]).astype(i32)

    own, away = factors(place, adapter_down_factors[0].T, adapter_up_factors[0])
    facing = lax.ppermute(away, AXES, pairs_of(lambda xl, y, xh, z, c: (1 - xl, y, 1 - xh, z, c)))
    ring = pairs_of(lambda xl, y, xh, z, c: (xl, y, xh, z + 1 - 2 * c, c))
    a = join([own, shift(own, "c", 1)])
    b = join([facing, shift(facing, "c", 1)])
    held = [own, facing]
    for step in range(1, 5):
        a = lax.ppermute(a if step < 4 else head(a, rank), AXES, ring)
        b = lax.ppermute(b if step < 4 else head(b, rank), AXES, ring)
        held += [a, b]

    id_hot = (token_adapter_index == columns[None, :]).astype(i32)
    slot_ids = jnp.sum(id_hot * placement[None, :], axis=1)
    id_rows = jnp.broadcast_to(slot_ids.astype(bf16)[None, :], (8, rows))
    packed = pack(tokens, id_rows)
    mine = exchange(packed, XRING).reshape(4 * rows, part + LANES)
    other = shift(mine, "c", 1)

    panels = spread_panels(place, base_key_weight.T)
    wide = panels.shape[1]
    base = exchange(panels, ("xl", "y")).reshape(16 * wide, part)

    low, up_first = low_product(rank, part, HELD[:8], place, held[:5], mine, other)
    low, up_second = low_product(rank, part, HELD[8:], place, held[5:], mine, other, low)
    out = base_product(place, base, mine, other, low)
    got = exchange(out, ("xh", "xl", "c"))
    other_first = shift(up_first, "c", 1)
    other_second = shift(up_second, "c", 1)
    ups = (up_first, up_second, other_first, other_second)
    return finish(rank, wide, place, got, ups, id_rows)


def solution(mesh):
    fine = Mesh(mesh.devices.reshape(SIZES), AXES)
    whole = ("xl", "y", "xh", "z", "c")
    adapter = ("xh", "z", "c")

    return jax.shard_map(
        on_device,
        mesh=fine,
        in_specs=(
            P(whole, None),
            P(None, ("xl", "y")),
            P(adapter, None, None),
            P(adapter, None, None),
            P(whole, None),
            P(),
        ),
        out_specs=P(whole, None),
        check_vma=False,
    )
```

profile of v0, /device:TPU:1, one launch (start us, length us, event | category | flops | bytes accessed | tf_op | source)
XLA Modules:
  0.0 159.8 jit_solution(1010039834010806515)
XLA Ops:
  0.8 1.6 copy-done.4
  2.8 1.4 copy-done
  4.2 5.0 %all-to-all-start.1 = ((bf16[4,128,2176]{2,1,0:T(8,128)(2,1)}), bf16[4,128,2176]{2,1,0:T(8,128)(2,1)S(1)}, u32[]{:S(2)}, u32[]{:S(2)}) async-start(bf16[4,128,2176]{2,1,0:T(8,128)(2,1)} %copy-done), calls=%async_computation.1 | async-start | bytes 4456448 | tf_op jit(solution)/shard_map/all_to_all | solution.py:43
  10.6 4.6 %collective-permute-start.1 = (bf16[64,2816]{1,0:T(8,128)(2,1)S(1)}, bf16[64,2816]{1,0:T(8,128)(2,1)S(1)}, u32[]{:S(2)}, u32[]{:S(2)}) collective-permute-start(bf16[64,2816]{1,0:T(8,128)(2,1)S(1)} %get-tuple-element.11), channel_id=1, source_target_pairs={{0,272},{1,273},{2,274},{3,275},{4,276},{5,277},{6,278},{7,279},{8... | collective-permute-start | bytes 1081352 | tf_op jit(solution)/shard_map/ppermute | solution.py:304
  15.1 8.1 %collective-permute-start.5 = (bf16[64,2816]{1,0:T(8,128)(2,1)}, bf16[64,2816]{1,0:T(8,128)(2,1)S(1)}, u32[]{:S(2)}, u32[]{:S(2)}) collective-permute-start(bf16[64,2816]{1,0:T(8,128)(2,1)} %get-tuple-element.12.refs_0_), channel_id=1, source_target_pairs={{0,1},{1,0},{2,3},{3,2},{4,5},{5,4},{6,7},{7,6},{8,9},{9,8},{10,11... | collective-permute-start | bytes 1081352 | tf_op jit(solution)/shard_map/ppermute | solution.py:39
  23.2 15.6 %collective-permute-done.1.refs_0_.refs_1_ = bf16[64,2816]{1,0:T(8,128)(2,1)S(1)} collective-permute-done((bf16[64,2816]{1,0:T(8,128)(2,1)S(1)}, bf16[64,2816]{1,0:T(8,128)(2,1)S(1)}, u32[]{:S(2)}, u32[]{:S(2)}) %collective-permute-start.1) | collective-permute-done | bytes 360480 | tf_op jit(solution)/shard_map/ppermute | solution.py:304
  38.8 8.4 %collective-permute-start.2 = (bf16[64,2816]{1,0:T(8,128)(2,1)S(1)}, bf16[64,2816]{1,0:T(8,128)(2,1)S(1)}, u32[]{:S(2)}, u32[]{:S(2)}) collective-permute-start(bf16[64,2816]{1,0:T(8,128)(2,1)S(1)} %collective-permute-done.1.refs_0_.refs_1_), channel_id=1, source_target_pairs={{0,1},{1,0},{2,3},{3,2},{4,5},{5,4},{6,7},{7,6},{8,9},{9,8},{10,11... | collective-permute-start | bytes 1081352 | tf_op jit(solution)/shard_map/ppermute | solution.py:39
  50.1 7.0 %all-to-all-start = ((bf16[16,24,2048]{2,1,0:T(8,128)(2,1)}), bf16[16,24,2048]{2,1,0:T(8,128)(2,1)}, u32[]{:S(2)}, u32[]{:S(2)}) async-start(bf16[16,24,2048]{2,1,0:T(8,128)(2,1)} %copy-done.1), calls=%async_computation | async-start | bytes 3145728 | tf_op jit(solution)/shard_map/all_to_all | solution.py:43
  58.2 10.7 %collective-permute-start.6 = (bf16[128,2816]{1,0:T(8,128)(2,1)S(1)}, bf16[128,2816]{1,0:T(8,128)(2,1)S(1)}, u32[]{:S(2)}, u32[]{:S(2)}) collective-permute-start(bf16[128,2816]{1,0:T(8,128)(2,1)S(1)} %join.3), channel_id=1, source_target_pairs={{0,2},{1,15},{2,4},{3,1},{4,6},{5,3},{6,8},{7,5},{8,10},{9,7},{10,... | collective-permute-start | bytes 2162696 | tf_op jit(solution)/shard_map/ppermute | solution.py:310
  68.9 2.2 %collective-permute-start.3 = (bf16[128,2816]{1,0:T(8,128)(2,1)S(1)}, bf16[128,2816]{1,0:T(8,128)(2,1)S(1)}, u32[]{:S(2)}, u32[]{:S(2)}) collective-permute-start(bf16[128,2816]{1,0:T(8,128)(2,1)S(1)} %join.2), channel_id=1, source_target_pairs={{0,2},{1,15},{2,4},{3,1},{4,6},{5,3},{6,8},{7,5},{8,10},{9,7},{10,... | collective-permute-start | bytes 2162696 | tf_op jit(solution)/shard_map/ppermute | solution.py:311
  71.1 1.9 %collective-permute-start = (bf16[512,2176]{1,0:T(8,128)(2,1)S(1)}, bf16[512,2176]{1,0:T(8,128)(2,1)S(1)}, u32[]{:S(2)}, u32[]{:S(2)}) collective-permute-start(bf16[512,2176]{1,0:T(8,128)(2,1)S(1)} %bitcast.13), channel_id=1, source_target_pairs={{0,1},{1,0},{2,3},{3,2},{4,5},{5,4},{6,7},{7,6},{8,9},{9,8},{10,11... | collective-permute-start | bytes 6684680 | tf_op jit(solution)/shard_map/ppermute | solution.py:39
  73.0 4.0 %collective-permute-done.6.refs_2_ = bf16[128,2816]{1,0:T(8,128)(2,1)S(1)} collective-permute-done((bf16[128,2816]{1,0:T(8,128)(2,1)S(1)}, bf16[128,2816]{1,0:T(8,128)(2,1)S(1)}, u32[]{:S(2)}, u32[]{:S(2)}) %collective-permute-start.6) | collective-permute-done | bytes 720928 | tf_op jit(solution)/shard_map/ppermute | solution.py:310
  77.0 5.3 %collective-permute-start.7 = (bf16[128,2816]{1,0:T(8,128)(2,1)S(1)}, bf16[128,2816]{1,0:T(8,128)(2,1)S(1)}, u32[]{:S(2)}, u32[]{:S(2)}) collective-permute-start(bf16[128,2816]{1,0:T(8,128)(2,1)S(1)} %collective-permute-done.6.refs_2_), channel_id=1, source_target_pairs={{0,2},{1,15},{2,4},{3,1},{4,6},{5,3},{6,8},{7,5},{8,10},{9,7},{10,... | collective-permute-start | bytes 2162696 | tf_op jit(solution)/shard_map/ppermute | solution.py:310
  82.3 2.5 %collective-permute-done.3.refs_3_ = bf16[128,2816]{1,0:T(8,128)(2,1)S(1)} collective-permute-done((bf16[128,2816]{1,0:T(8,128)(2,1)S(1)}, bf16[128,2816]{1,0:T(8,128)(2,1)S(1)}, u32[]{:S(2)}, u32[]{:S(2)}) %collective-permute-start.3) | collective-permute-done | bytes 720928 | tf_op jit(solution)/shard_map/ppermute | solution.py:311
  84.8 5.3 %collective-permute-start.4 = (bf16[128,2816]{1,0:T(8,128)(2,1)S(1)}, bf16[128,2816]{1,0:T(8,128)(2,1)S(1)}, u32[]{:S(2)}, u32[]{:S(2)}) collective-permute-start(bf16[128,2816]{1,0:T(8,128)(2,1)S(1)} %collective-permute-done.3.refs_3_), channel_id=1, source_target_pairs={{0,2},{1,15},{2,4},{3,1},{4,6},{5,3},{6,8},{7,5},{8,10},{9,7},{10,... | collective-permute-start | bytes 2162696 | tf_op jit(solution)/shard_map/ppermute | solution.py:311
  90.0 2.5 %collective-permute-done.7.refs_4_ = bf16[128,2816]{1,0:T(8,128)(2,1)S(1)} collective-permute-done((bf16[128,2816]{1,0:T(8,128)(2,1)S(1)}, bf16[128,2816]{1,0:T(8,128)(2,1)S(1)}, u32[]{:S(2)}, u32[]{:S(2)}) %collective-permute-start.7) | collective-permute-done | bytes 720928 | tf_op jit(solution)/shard_map/ppermute | solution.py:310
  92.5 5.3 %collective-permute-start.8 = (bf16[128,2816]{1,0:T(8,128)(2,1)S(1)}, bf16[128,2816]{1,0:T(8,128)(2,1)S(1)}, u32[]{:S(2)}, u32[]{:S(2)}) collective-permute-start(bf16[128,2816]{1,0:T(8,128)(2,1)S(1)} %collective-permute-done.7.refs_4_), channel_id=1, source_target_pairs={{0,2},{1,15},{2,4},{3,1},{4,6},{5,3},{6,8},{7,5},{8,10},{9,7},{10,... | collective-permute-start | bytes 2162696 | tf_op jit(solution)/shard_map/ppermute | solution.py:310
  97.8 2.5 %collective-permute-done.4.refs_0_ = bf16[128,2816]{1,0:T(8,128)(2,1)S(1)} collective-permute-done((bf16[128,2816]{1,0:T(8,128)(2,1)S(1)}, bf16[128,2816]{1,0:T(8,128)(2,1)S(1)}, u32[]{:S(2)}, u32[]{:S(2)}) %collective-permute-start.4) | collective-permute-done | bytes 720928 | tf_op jit(solution)/shard_map/ppermute | solution.py:311
  100.2 5.4 %collective-permute-start.9 = (bf16[128,2816]{1,0:T(8,128)(2,1)S(1)}, bf16[128,2816]{1,0:T(8,128)(2,1)S(1)}, u32[]{:S(2)}, u32[]{:S(2)}) collective-permute-start(bf16[128,2816]{1,0:T(8,128)(2,1)S(1)} %collective-permute-done.4.refs_0_), channel_id=1, source_target_pairs={{0,2},{1,15},{2,4},{3,1},{4,6},{5,3},{6,8},{7,5},{8,10},{9,7},{10,... | collective-permute-start | bytes 2162696 | tf_op jit(solution)/shard_map/ppermute | solution.py:311
  105.6 2.3 %collective-permute-done.8.ref.refs_1_ = bf16[128,2816]{1,0:T(8,128)(2,1)S(1)} collective-permute-done((bf16[128,2816]{1,0:T(8,128)(2,1)S(1)}, bf16[128,2816]{1,0:T(8,128)(2,1)S(1)}, u32[]{:S(2)}, u32[]{:S(2)}) %collective-permute-start.8) | collective-permute-done | bytes 720928 | tf_op jit(solution)/shard_map/ppermute | solution.py:310
  108.0 5.0 %collective-permute-start.10 = (bf16[64,2816]{1,0:T(8,128)(2,1)S(1)}, bf16[64,2816]{1,0:T(8,128)(2,1)S(1)}, u32[]{:S(2)}, u32[]{:S(2)}) collective-permute-start(bf16[64,2816]{1,0:T(8,128)(2,1)S(1)} %head.2), channel_id=1, source_target_pairs={{0,2},{1,15},{2,4},{3,1},{4,6},{5,3},{6,8},{7,5},{8,10},{9,7},{10,... | collective-permute-start | bytes 1081352 | tf_op jit(solution)/shard_map/ppermute | solution.py:310
  113.0 2.7 %collective-permute-done.9.ref.refs_2_ = bf16[128,2816]{1,0:T(8,128)(2,1)S(1)} collective-permute-done((bf16[128,2816]{1,0:T(8,128)(2,1)S(1)}, bf16[128,2816]{1,0:T(8,128)(2,1)S(1)}, u32[]{:S(2)}, u32[]{:S(2)}) %collective-permute-start.9) | collective-permute-done | bytes 720928 | tf_op jit(solution)/shard_map/ppermute | solution.py:311
  115.7 5.0 %collective-permute-start.11 = (bf16[64,2816]{1,0:T(8,128)(2,1)S(1)}, bf16[64,2816]{1,0:T(8,128)(2,1)S(1)}, u32[]{:S(2)}, u32[]{:S(2)}) collective-permute-start(bf16[64,2816]{1,0:T(8,128)(2,1)S(1)} %head.3), channel_id=1, source_target_pairs={{0,2},{1,15},{2,4},{3,1},{4,6},{5,3},{6,8},{7,5},{8,10},{9,7},{10,... | collective-permute-start | bytes 1081352 | tf_op jit(solution)/shard_map/ppermute | solution.py:311
  120.7 3.7 %low_product.2 = (f32[2,64,512]{2,1,0:T(8,128)S(1)}, bf16[512,768]{1,0:T(8,128)(2,1)S(1)}) custom-call(s32[5]{0:T(128)S(1)} %stack.23.place, bf16[64,2816]{1,0:T(8,128)(2,1)} %get-tuple-element.12.refs_0_, bf16[64,2816]{1,0:T(8,128)(2,1)S(1)} %collective-permute-done.1.refs_0_.refs_1_, bf16[128,2816]{1,0:T(8,128)(2,1)S(1)} %collective-permute-done.6.refs_2_, ...), custom_call_target="tpu_custom_call" | custom-call | flops 2147483648 | bytes 2097152 | tf_op jit(solution)/shard_map/low_product/pallas_call | solution.py:241
  125.1 3.0 %low_product.3 = (bf16[8,64,128]{2,1,0:T(8,128)(2,1)S(1)}, bf16[512,768]{1,0:T(8,128)(2,1)S(1)}) custom-call(s32[5]{0:T(128)S(1)} %stack.23.place, bf16[128,2816]{1,0:T(8,128)(2,1)S(1)} %collective-permute-done.4.refs_0_, bf16[128,2816]{1,0:T(8,128)(2,1)S(1)} %collective-permute-done.8.ref.refs_1_, bf16[128,2816]{1,0:T(8,128)(2,1)S(1)} %collective-permute-done.9.ref.refs_2_, ...), custom_call_target="tpu_custom_call" | custom-call | flops 2147483648 | bytes 2097152 | tf_op jit(solution)/shard_map/low_product/pallas_call | solution.py:241
  129.0 1.6 %copy-done.3 = bf16[512,2176]{1,0:T(8,128)(2,1)S(1)} copy-done((bf16[512,2176]{1,0:T(8,128)(2,1)S(1)}, bf16[512,2176]{1,0:T(8,128)(2,1)}, u32[]{:S(2)}) %copy-start.3) | copy-done | bytes 2228248
  130.6 4.2 %base_product.1 = bf16[8,448,128]{2,1,0:T(8,128)(2,1)} custom-call(s32[5]{0:T(128)S(1)} %stack.23.place, bf16[384,2048]{1,0:T(8,128)(2,1)} %bitcast.6.base, bf16[512,2176]{1,0:T(8,128)(2,1)S(1)} %bitcast.16, bf16[512,2176]{1,0:T(8,128)(2,1)S(1)} %copy-done.3, bf16[8,64,128]{2,1,0:T(8,128)(2,1)S(1)} %get-tuple-element.14.low), custom_call_target="tpu_custom_call" | custom-call | flops 1610612736 | bytes 6029312 | tf_op jit(solution)/shard_map/base_product/pallas_call | solution.py:196
  134.8 6.2 %all-to-all-start.2 = ((bf16[8,448,128]{2,1,0:T(8,128)(2,1)}), bf16[8,448,128]{2,1,0:T(8,128)(2,1)S(1)}, u32[]{:S(2)}, u32[]{:S(2)}) async-start(bf16[8,448,128]{2,1,0:T(8,128)(2,1)} %base_product.1), calls=%async_computation.2 | async-start | bytes 1835008 | tf_op jit(solution)/shard_map/all_to_all | solution.py:43
  141.0 2.0 %collective-permute-start.13 = (bf16[512,768]{1,0:T(8,128)(2,1)}, bf16[512,768]{1,0:T(8,128)(2,1)S(1)}, u32[]{:S(2)}, u32[]{:S(2)}) collective-permute-start(bf16[512,768]{1,0:T(8,128)(2,1)} %copy-done.7), channel_id=1, source_target_pairs={{0,1},{1,0},{2,3},{3,2},{4,5},{5,4},{6,7},{7,6},{8,9},{9,8},{10,11... | collective-permute-start | bytes 2359304 | tf_op jit(solution)/shard_map/ppermute | solution.py:39
  143.0 2.3 %collective-permute-start.12 = (bf16[512,768]{1,0:T(8,128)(2,1)S(1)}, bf16[512,768]{1,0:T(8,128)(2,1)S(1)}, u32[]{:S(2)}, u32[]{:S(2)}) collective-permute-start(bf16[512,768]{1,0:T(8,128)(2,1)S(1)} %get-tuple-element.15.u_mine0), channel_id=1, source_target_pairs={{0,1},{1,0},{2,3},{3,2},{4,5},{5,4},{6,7},{7,6},{8,9},{9,8},{10,11... | collective-permute-start | bytes 2359304 | tf_op jit(solution)/shard_map/ppermute | solution.py:39
  148.1 6.5 %all-to-all-done.2.got = bf16[8,448,128]{2,1,0:T(8,128)(2,1)S(1)} async-done(((bf16[8,448,128]{2,1,0:T(8,128)(2,1)}), bf16[8,448,128]{2,1,0:T(8,128)(2,1)S(1)}, u32[]{:S(2)}, u32[]{:S(2)}) %all-to-all-start.2) | async-done | bytes 917536 | tf_op jit(solution)/shard_map/all_to_all | solution.py:43
  158.0 1.9 %finish.1 = bf16[128,768]{1,0:T(8,128)(2,1)} custom-call(s32[5]{0:T(128)S(1)} %stack.23.place, bf16[8,448,128]{2,1,0:T(8,128)(2,1)S(1)} %all-to-all-done.2.got, bf16[512,768]{1,0:T(8,128)(2,1)S(1)} %get-tuple-element.15.u_mine0, bf16[512,768]{1,0:T(8,128)(2,1)S(1)} %copy-done.8, bf16[512,768]{1,0:T(8,128)(2,1)S(1)} %copy-done.12, ...), custom_call_target="tpu_custom_call" | custom-call | flops 402653184 | bytes 917504 | tf_op jit(solution)/shard_map/finish/pallas_call | solution.py:282
  (45 shorter events, 14.4 us)
Async XLA Ops:
  0.8 1.6 copy-start.4
  2.8 1.4 copy-start
  4.2 5.1 %copy-start.5 = (bf16[1,8192,64]{1,2,0:T(8,128)(2,1)S(1)}, bf16[1,8192,64]{1,2,0:T(8,128)(2,1)}, u32[]{:S(2)}) copy-start(bf16[1,8192,64]{1,2,0:T(8,128)(2,1)} %param.8) | copy-start | bytes 3145732
  4.2 5.1 %copy-start.13 = (bf16[1,64,768]{2,1,0:T(8,128)(2,1)S(1)}, bf16[1,64,768]{2,1,0:T(8,128)(2,1)}, u32[]{:S(2)}) copy-start(bf16[1,64,768]{2,1,0:T(8,128)(2,1)} %param.9) | copy-start | bytes 294916
  4.2 46.0 %all-to-all-start.1 = ((bf16[4,128,2176]{2,1,0:T(8,128)(2,1)}), bf16[4,128,2176]{2,1,0:T(8,128)(2,1)S(1)}, u32[]{:S(2)}, u32[]{:S(2)}) async-start(bf16[4,128,2176]{2,1,0:T(8,128)(2,1)} %copy-done), calls=%async_computation.1 | async-start | bytes 4456448 | tf_op jit(solution)/shard_map/all_to_all | solution.py:43
  10.6 28.2 %collective-permute-start.1 = (bf16[64,2816]{1,0:T(8,128)(2,1)S(1)}, bf16[64,2816]{1,0:T(8,128)(2,1)S(1)}, u32[]{:S(2)}, u32[]{:S(2)}) collective-permute-start(bf16[64,2816]{1,0:T(8,128)(2,1)S(1)} %get-tuple-element.11), channel_id=1, source_target_pairs={{0,272},{1,273},{2,274},{3,275},{4,276},{5,277},{6,278},{7,279},{8... | collective-permute-start | bytes 1081352 | tf_op jit(solution)/shard_map/ppermute | solution.py:304
  15.1 42.0 %collective-permute-start.5 = (bf16[64,2816]{1,0:T(8,128)(2,1)}, bf16[64,2816]{1,0:T(8,128)(2,1)S(1)}, u32[]{:S(2)}, u32[]{:S(2)}) collective-permute-start(bf16[64,2816]{1,0:T(8,128)(2,1)} %get-tuple-element.12.refs_0_), channel_id=1, source_target_pairs={{0,1},{1,0},{2,3},{3,2},{4,5},{5,4},{6,7},{7,6},{8,9},{9,8},{10,11... | collective-permute-start | bytes 1081352 | tf_op jit(solution)/shard_map/ppermute | solution.py:39
  38.8 30.0 %collective-permute-start.2 = (bf16[64,2816]{1,0:T(8,128)(2,1)S(1)}, bf16[64,2816]{1,0:T(8,128)(2,1)S(1)}, u32[]{:S(2)}, u32[]{:S(2)}) collective-permute-start(bf16[64,2816]{1,0:T(8,128)(2,1)S(1)} %collective-permute-done.1.refs_0_.refs_1_), channel_id=1, source_target_pairs={{0,1},{1,0},{2,3},{3,2},{4,5},{5,4},{6,7},{7,6},{8,9},{9,8},{10,11... | collective-permute-start | bytes 1081352 | tf_op jit(solution)/shard_map/ppermute | solution.py:39
  47.2 1.1 copy-start.6
  49.0 1.2 copy-start.1
  50.1 78.8 %all-to-all-start = ((bf16[16,24,2048]{2,1,0:T(8,128)(2,1)}), bf16[16,24,2048]{2,1,0:T(8,128)(2,1)}, u32[]{:S(2)}, u32[]{:S(2)}) async-start(bf16[16,24,2048]{2,1,0:T(8,128)(2,1)} %copy-done.1), calls=%async_computation | async-start | bytes 3145728 | tf_op jit(solution)/shard_map/all_to_all | solution.py:43
  58.2 18.9 %collective-permute-start.6 = (bf16[128,2816]{1,0:T(8,128)(2,1)S(1)}, bf16[128,2816]{1,0:T(8,128)(2,1)S(1)}, u32[]{:S(2)}, u32[]{:S(2)}) collective-permute-start(bf16[128,2816]{1,0:T(8,128)(2,1)S(1)} %join.3), channel_id=1, source_target_pairs={{0,2},{1,15},{2,4},{3,1},{4,6},{5,3},{6,8},{7,5},{8,10},{9,7},{10,... | collective-permute-start | bytes 2162696 | tf_op jit(solution)/shard_map/ppermute | solution.py:310
  68.9 15.9 %collective-permute-start.3 = (bf16[128,2816]{1,0:T(8,128)(2,1)S(1)}, bf16[128,2816]{1,0:T(8,128)(2,1)S(1)}, u32[]{:S(2)}, u32[]{:S(2)}) collective-permute-start(bf16[128,2816]{1,0:T(8,128)(2,1)S(1)} %join.2), channel_id=1, source_target_pairs={{0,2},{1,15},{2,4},{3,1},{4,6},{5,3},{6,8},{7,5},{8,10},{9,7},{10,... | collective-permute-start | bytes 2162696 | tf_op jit(solution)/shard_map/ppermute | solution.py:311
  71.1 49.6 %collective-permute-start = (bf16[512,2176]{1,0:T(8,128)(2,1)S(1)}, bf16[512,2176]{1,0:T(8,128)(2,1)S(1)}, u32[]{:S(2)}, u32[]{:S(2)}) collective-permute-start(bf16[512,2176]{1,0:T(8,128)(2,1)S(1)} %bitcast.13), channel_id=1, source_target_pairs={{0,1},{1,0},{2,3},{3,2},{4,5},{5,4},{6,7},{7,6},{8,9},{9,8},{10,11... | collective-permute-start | bytes 6684680 | tf_op jit(solution)/shard_map/ppermute | solution.py:39
  77.0 15.4 %collective-permute-start.7 = (bf16[128,2816]{1,0:T(8,128)(2,1)S(1)}, bf16[128,2816]{1,0:T(8,128)(2,1)S(1)}, u32[]{:S(2)}, u32[]{:S(2)}) collective-permute-start(bf16[128,2816]{1,0:T(8,128)(2,1)S(1)} %collective-permute-done.6.refs_2_), channel_id=1, source_target_pairs={{0,2},{1,15},{2,4},{3,1},{4,6},{5,3},{6,8},{7,5},{8,10},{9,7},{10,... | collective-permute-start | bytes 2162696 | tf_op jit(solution)/shard_map/ppermute | solution.py:310
  84.8 15.4 %collective-permute-start.4 = (bf16[128,2816]{1,0:T(8,128)(2,1)S(1)}, bf16[128,2816]{1,0:T(8,128)(2,1)S(1)}, u32[]{:S(2)}, u32[]{:S(2)}) collective-permute-start(bf16[128,2816]{1,0:T(8,128)(2,1)S(1)} %collective-permute-done.3.refs_3_), channel_id=1, source_target_pairs={{0,2},{1,15},{2,4},{3,1},{4,6},{5,3},{6,8},{7,5},{8,10},{9,7},{10,... | collective-permute-start | bytes 2162696 | tf_op jit(solution)/shard_map/ppermute | solution.py:311
  92.5 15.4 %collective-permute-start.8 = (bf16[128,2816]{1,0:T(8,128)(2,1)S(1)}, bf16[128,2816]{1,0:T(8,128)(2,1)S(1)}, u32[]{:S(2)}, u32[]{:S(2)}) collective-permute-start(bf16[128,2816]{1,0:T(8,128)(2,1)S(1)} %collective-permute-done.7.refs_4_), channel_id=1, source_target_pairs={{0,2},{1,15},{2,4},{3,1},{4,6},{5,3},{6,8},{7,5},{8,10},{9,7},{10,... | collective-permute-start | bytes 2162696 | tf_op jit(solution)/shard_map/ppermute | solution.py:310
  100.2 15.4 %collective-permute-start.9 = (bf16[128,2816]{1,0:T(8,128)(2,1)S(1)}, bf16[128,2816]{1,0:T(8,128)(2,1)S(1)}, u32[]{:S(2)}, u32[]{:S(2)}) collective-permute-start(bf16[128,2816]{1,0:T(8,128)(2,1)S(1)} %collective-permute-done.4.refs_0_), channel_id=1, source_target_pairs={{0,2},{1,15},{2,4},{3,1},{4,6},{5,3},{6,8},{7,5},{8,10},{9,7},{10,... | collective-permute-start | bytes 2162696 | tf_op jit(solution)/shard_map/ppermute | solution.py:311
  108.0 16.5 %collective-permute-start.10 = (bf16[64,2816]{1,0:T(8,128)(2,1)S(1)}, bf16[64,2816]{1,0:T(8,128)(2,1)S(1)}, u32[]{:S(2)}, u32[]{:S(2)}) collective-permute-start(bf16[64,2816]{1,0:T(8,128)(2,1)S(1)} %head.2), channel_id=1, source_target_pairs={{0,2},{1,15},{2,4},{3,1},{4,6},{5,3},{6,8},{7,5},{8,10},{9,7},{10,... | collective-permute-start | bytes 1081352 | tf_op jit(solution)/shard_map/ppermute | solution.py:310
  115.7 9.4 %collective-permute-start.11 = (bf16[64,2816]{1,0:T(8,128)(2,1)S(1)}, bf16[64,2816]{1,0:T(8,128)(2,1)S(1)}, u32[]{:S(2)}, u32[]{:S(2)}) collective-permute-start(bf16[64,2816]{1,0:T(8,128)(2,1)S(1)} %head.3), channel_id=1, source_target_pairs={{0,2},{1,15},{2,4},{3,1},{4,6},{5,3},{6,8},{7,5},{8,10},{9,7},{10,... | collective-permute-start | bytes 1081352 | tf_op jit(solution)/shard_map/ppermute | solution.py:311
  120.7 4.3 %copy-start.2 = (bf16[512,2176]{1,0:T(8,128)(2,1)}, bf16[512,2176]{1,0:T(8,128)(2,1)S(1)}, u32[]{:S(2)}) copy-start(bf16[512,2176]{1,0:T(8,128)(2,1)S(1)} %collective-permute-done.refs_6_.other) | copy-start | bytes 6684676
  128.0 0.9 copy-start.7
  129.0 1.6 %copy-start.3 = (bf16[512,2176]{1,0:T(8,128)(2,1)S(1)}, bf16[512,2176]{1,0:T(8,128)(2,1)}, u32[]{:S(2)}) copy-start(bf16[512,2176]{1,0:T(8,128)(2,1)} %copy-done.2) | copy-start | bytes 6684676
  134.8 19.8 %all-to-all-start.2 = ((bf16[8,448,128]{2,1,0:T(8,128)(2,1)}), bf16[8,448,128]{2,1,0:T(8,128)(2,1)S(1)}, u32[]{:S(2)}, u32[]{:S(2)}) async-start(bf16[8,448,128]{2,1,0:T(8,128)(2,1)} %base_product.1), calls=%async_computation.2 | async-start | bytes 1835008 | tf_op jit(solution)/shard_map/all_to_all | solution.py:43
  141.0 4.4 %collective-permute-start.13 = (bf16[512,768]{1,0:T(8,128)(2,1)}, bf16[512,768]{1,0:T(8,128)(2,1)S(1)}, u32[]{:S(2)}, u32[]{:S(2)}) collective-permute-start(bf16[512,768]{1,0:T(8,128)(2,1)} %copy-done.7), channel_id=1, source_target_pairs={{0,1},{1,0},{2,3},{3,2},{4,5},{5,4},{6,7},{7,6},{8,9},{9,8},{10,11... | collective-permute-start | bytes 2359304 | tf_op jit(solution)/shard_map/ppermute | solution.py:39
  143.0 4.2 %collective-permute-start.12 = (bf16[512,768]{1,0:T(8,128)(2,1)S(1)}, bf16[512,768]{1,0:T(8,128)(2,1)S(1)}, u32[]{:S(2)}, u32[]{:S(2)}) collective-permute-start(bf16[512,768]{1,0:T(8,128)(2,1)S(1)} %get-tuple-element.15.u_mine0), channel_id=1, source_target_pairs={{0,1},{1,0},{2,3},{3,2},{4,5},{5,4},{6,7},{7,6},{8,9},{9,8},{10,11... | collective-permute-start | bytes 2359304 | tf_op jit(solution)/shard_map/ppermute | solution.py:39
  145.4 0.9 copy-start.9
  147.2 0.9 copy-start.11
  154.6 1.1 copy-start.8
  155.7 1.1 copy-start.10
  156.8 1.1 copy-start.12
where the time goes:
time: 161 us; the launch traced here: 160 us
  starting transfers between devices  89.5 us (56%)
  waiting for transfers between devices  40.1 us (25%)
  Pallas kernels  16.2 us (10%)
  local copies, waits for them, and re-layouts  13.1 us (8%)
    ppermute x4, starting transfers between devices, on_device(): a = lax.ppermute(a if step < 4 else head(a, rank), AXES, ring)  26.2 us
    ppermute x5, starting transfers between devices, shift(): return lax.ppermute(value, axis, [(i, (i + by) % n) for i in range(n)])  22.7 us
    all_to_all x3, starting transfers between devices, exchange(): return lax.all_to_all(value, axes, split_axis=0, concat_axis=0, tiled=True)  18.2 us
    ppermute x4, starting transfers between devices, on_device(): b = lax.ppermute(b if step < 4 else head(b, rank), AXES, ring)  17.9 us
    ppermute x1, waiting for transfers between devices, on_device(): lax.ppermute(away, AXES, pairs_of(lambda xl, y, xh, z, c: (1 - xl, y, 1 -...  15.6 us
    unnamed x28, local copies, waits for them, and re-layouts  13 us
    ppermute x4, waiting for transfers between devices, on_device(): a = lax.ppermute(a if step < 4 else head(a, rank), AXES, ring)  8.79 us
    ppermute x4, waiting for transfers between devices, on_device(): b = lax.ppermute(b if step < 4 else head(b, rank), AXES, ring)  8.23 us
  transfers between devices with their start and end apart: 17, of which 10 were waited for; matrix products, arithmetic and copies ran while one was open for 0% of the time, Pallas kernels for 6%

commit v1 on v0

--- a/solution.py
+++ b/solution.py
@@ -17,6 +17,7 @@
 i32 = jnp.int32
 VMEM = pl.BlockSpec(memory_space=pltpu.VMEM)
 SMEM = pl.BlockSpec(memory_space=pltpu.SMEM)
+HBM = pl.BlockSpec(memory_space=pltpu.HBM)
 
 
 def pairs_of(move):
@@ -180,10 +181,14 @@
     return jnp.concatenate([ref[s * LANES:s * LANES + 8, part:] for s in range(4)], axis=1)[0:1].astype(f32)
 
 
-def base_kernel(place, base, mine, other, low, out):
+def base_kernel(place, base, mine, other, low, out, near, sem):
     cols, rows = base.shape[0], out.shape[2]
+    copy = pltpu.make_async_copy(mine, near, sem)
+    copy.start()
     out[:, cols:, :] = low[...]
-    for o, ref in enumerate((mine, other)):
+    for o, ref in ((1, other), (0, near)):
+        if o == 0:
+            copy.wait()
         at = jnp.bitwise_xor(place[4], o)
         product = nt(base[...], token_rows(ref)).astype(bf16)
         for x in range(4):
@@ -195,9 +200,10 @@
     toks = mine.shape[0]
     return pl.pallas_call(
         base_kernel,
-        in_specs=[SMEM] + [VMEM] * 4,
+        in_specs=[SMEM, VMEM, HBM, VMEM, VMEM],
         out_specs=VMEM,
         out_shape=jax.ShapeDtypeStruct((8, cols + low.shape[1], toks // 4), bf16),
+        scratch_shapes=[pltpu.VMEM(mine.shape, bf16), pltpu.SemaphoreType.DMA(())],
         cost_estimate=cost(4 * cols * part * toks, 2 * (base.size + 2 * mine.size)),
         compiler_params=params(20),
         name="base_product",
@@ -249,7 +255,11 @@
     )(place, *operands)
 
 
-def final_kernel(rank, wide, place, got, u_mine0, u_mine1, u_other0, u_other1, ids, out):
+def final_kernel(rank, wide, place, got, u_mine0, u_mine1, u_other0, u_other1, ids, out, near, sems):
+    order = ((0, 0, u_mine0), (1, 0, u_other0), (0, 1, u_mine1), (1, 1, u_other1))
+    copies = [pltpu.make_async_copy(u, near.at[i], sems.at[i]) for i, (_, _, u) in enumerate(order)]
+    for copy in copies:
+        copy.start()
     rows = got.shape[2]
     cols = got.shape[1] - rank
     base = []
@@ -266,13 +276,14 @@
     low = low.astype(bf16).astype(f32)
     names = ids[0:1, :].astype(f32)
     delta = None
-    for o, k, u in ((0, 0, u_mine0), (1, 0, u_other0), (0, 1, u_mine1), (1, 1, u_other1)):
+    for i, (o, k, _) in enumerate(order):
         core = 1 - place[4] if o else place[4]
         entries = HELD[8 * k:8 * k + 8]
         spread = jnp.concatenate(
             [jnp.where(names == slot_of(place, entry, core), low, 0.0) for entry in entries], axis=0
         )
-        term = jnp.dot(spread.T.astype(bf16), u[...], preferred_element_type=f32)
+        copies[i].wait()
+        term = jnp.dot(spread.T.astype(bf16), near[i], preferred_element_type=f32)
         delta = term if delta is None else delta + term
     out[...] = (base.T + delta.astype(bf16).astype(f32)).astype(bf16)
 
@@ -281,11 +292,12 @@
     rows = got.shape[2]
     return pl.pallas_call(
         functools.partial(final_kernel, rank, wide),
-        in_specs=[SMEM] + [VMEM] * 6,
-        out_specs=VMEM,
+        in_specs=[SMEM, VMEM] + [HBM] * 4 + [VMEM],
+        out_specs=VMEM,
+        scratch_shapes=[pltpu.VMEM((4,) + ups[0].shape, bf16), pltpu.SemaphoreType.DMA((4,))],
         out_shape=jax.ShapeDtypeStruct((rows, 2 * (got.shape[1] - rank)), bf16),
         cost_estimate=cost(8 * ups[0].size * rows, 2 * got.size),
-        compiler_params=params(20),
+        compiler_params=params(58),
         name="finish",
     )(place, got, *ups, ids)
 

time: 161 us -> 161 us (level)
  local copies, waits for them, and re-layouts: 13.1 us -> 8.86 us
  Pallas kernels: 16.2 us -> 19.1 us
  waiting for transfers between devices: 40.1 us -> 41.8 us
    unnamed x28, local copies, waits for them, and re-layouts: 13 us -> 8.77 us
    pallas_call x1, Pallas kernels: 1.86 us -> 4.24 us  [finish(): pl.pallas_call(functools.partial(final_kernel, rank, wide), in_specs=[SME...]
where the time goes in v1:
time: 161 us; the launch traced here: 160 us
  starting transfers between devices  89.5 us (56%)
  waiting for transfers between devices  41.8 us (26%)
  Pallas kernels  19.1 us (12%)
  local copies, waits for them, and re-layouts  8.86 us (6%)
    ppermute x4, starting transfers between devices, on_device(): a = lax.ppermute(a if step < 4 else head(a, rank), AXES, ring)  26.2 us
    ppermute x5, starting transfers between devices, shift(): return lax.ppermute(value, axis, [(i, (i + by) % n) for i in range(n)])  22.7 us
    all_to_all x3, starting transfers between devices, exchange(): return lax.all_to_all(value, axes, split_axis=0, concat_axis=0, tiled=True)  18.2 us
    ppermute x4, starting transfers between devices, on_device(): b = lax.ppermute(b if step < 4 else head(b, rank), AXES, ring)  17.9 us
    ppermute x1, waiting for transfers between devices, on_device(): lax.ppermute(away, AXES, pairs_of(lambda xl, y, xh, z, c: (1 - xl, y, 1 -...  15.6 us
    ppermute x4, waiting for transfers between devices, on_device(): a = lax.ppermute(a if step < 4 else head(a, rank), AXES, ring)  8.79 us
    unnamed x28, local copies, waits for them, and re-layouts  8.77 us
    ppermute x4, waiting for transfers between devices, on_device(): b = lax.ppermute(b if step < 4 else head(b, rank), AXES, ring)  8.21 us
  transfers between devices with their start and end apart: 17, of which 10 were waited for; matrix products, arithmetic and copies ran while one was open for 0% of the time, Pallas kernels for 6%

profile of v1, /device:TPU:1, one launch (start us, length us, event | category | flops | bytes accessed | tf_op | source)
XLA Modules:
  0.0 160.3 jit_solution(6458276887344113292)
XLA Ops:
  0.8 1.6 copy-done.4
  4.2 5.0 %all-to-all-start.1 = ((bf16[4,128,2176]{2,1,0:T(8,128)(2,1)}), bf16[4,128,2176]{2,1,0:T(8,128)(2,1)S(1)}, u32[]{:S(2)}, u32[]{:S(2)}) async-start(bf16[4,128,2176]{2,1,0:T(8,128)(2,1)} %copy-done), calls=%async_computation.1 | async-start | bytes 4456448 | tf_op jit(solution)/shard_map/all_to_all | solution.py:44
  10.6 4.6 %collective-permute-start.1 = (bf16[64,2816]{1,0:T(8,128)(2,1)S(1)}, bf16[64,2816]{1,0:T(8,128)(2,1)S(1)}, u32[]{:S(2)}, u32[]{:S(2)}) collective-permute-start(bf16[64,2816]{1,0:T(8,128)(2,1)S(1)} %get-tuple-element.11), channel_id=1, source_target_pairs={{0,272},{1,273},{2,274},{3,275},{4,276},{5,277},{6,278},{7,279},{8... | collective-permute-start | bytes 1081352 | tf_op jit(solution)/shard_map/ppermute | solution.py:316
  15.2 8.1 %collective-permute-start.5 = (bf16[64,2816]{1,0:T(8,128)(2,1)}, bf16[64,2816]{1,0:T(8,128)(2,1)S(1)}, u32[]{:S(2)}, u32[]{:S(2)}) collective-permute-start(bf16[64,2816]{1,0:T(8,128)(2,1)} %get-tuple-element.12.refs_0_), channel_id=1, source_target_pairs={{0,1},{1,0},{2,3},{3,2},{4,5},{5,4},{6,7},{7,6},{8,9},{9,8},{10,11... | collective-permute-start | bytes 1081352 | tf_op jit(solution)/shard_map/ppermute | solution.py:40
  23.2 15.6 %collective-permute-done.1.refs_0_.refs_1_ = bf16[64,2816]{1,0:T(8,128)(2,1)S(1)} collective-permute-done((bf16[64,2816]{1,0:T(8,128)(2,1)S(1)}, bf16[64,2816]{1,0:T(8,128)(2,1)S(1)}, u32[]{:S(2)}, u32[]{:S(2)}) %collective-permute-start.1) | collective-permute-done | bytes 360480 | tf_op jit(solution)/shard_map/ppermute | solution.py:316
  38.8 8.4 %collective-permute-start.2 = (bf16[64,2816]{1,0:T(8,128)(2,1)S(1)}, bf16[64,2816]{1,0:T(8,128)(2,1)S(1)}, u32[]{:S(2)}, u32[]{:S(2)}) collective-permute-start(bf16[64,2816]{1,0:T(8,128)(2,1)S(1)} %collective-permute-done.1.refs_0_.refs_1_), channel_id=1, source_target_pairs={{0,1},{1,0},{2,3},{3,2},{4,5},{5,4},{6,7},{7,6},{8,9},{9,8},{10,11... | collective-permute-start | bytes 1081352 | tf_op jit(solution)/shard_map/ppermute | solution.py:40
  50.1 7.0 %all-to-all-start = ((bf16[16,24,2048]{2,1,0:T(8,128)(2,1)}), bf16[16,24,2048]{2,1,0:T(8,128)(2,1)}, u32[]{:S(2)}, u32[]{:S(2)}) async-start(bf16[16,24,2048]{2,1,0:T(8,128)(2,1)} %copy-done.1), calls=%async_computation | async-start | bytes 3145728 | tf_op jit(solution)/shard_map/all_to_all | solution.py:44
  58.2 10.7 %collective-permute-start.6 = (bf16[128,2816]{1,0:T(8,128)(2,1)S(1)}, bf16[128,2816]{1,0:T(8,128)(2,1)S(1)}, u32[]{:S(2)}, u32[]{:S(2)}) collective-permute-start(bf16[128,2816]{1,0:T(8,128)(2,1)S(1)} %join.3), channel_id=1, source_target_pairs={{0,2},{1,15},{2,4},{3,1},{4,6},{5,3},{6,8},{7,5},{8,10},{9,7},{10,... | collective-permute-start | bytes 2162696 | tf_op jit(solution)/shard_map/ppermute | solution.py:322
  68.9 2.2 %collective-permute-start.3 = (bf16[128,2816]{1,0:T(8,128)(2,1)S(1)}, bf16[128,2816]{1,0:T(8,128)(2,1)S(1)}, u32[]{:S(2)}, u32[]{:S(2)}) collective-permute-start(bf16[128,2816]{1,0:T(8,128)(2,1)S(1)} %join.2), channel_id=1, source_target_pairs={{0,2},{1,15},{2,4},{3,1},{4,6},{5,3},{6,8},{7,5},{8,10},{9,7},{10,... | collective-permute-start | bytes 2162696 | tf_op jit(solution)/shard_map/ppermute | solution.py:323
  71.1 1.9 %collective-permute-start = (bf16[512,2176]{1,0:T(8,128)(2,1)S(1)}, bf16[512,2176]{1,0:T(8,128)(2,1)S(1)}, u32[]{:S(2)}, u32[]{:S(2)}) collective-permute-start(bf16[512,2176]{1,0:T(8,128)(2,1)S(1)} %bitcast.13), channel_id=1, source_target_pairs={{0,1},{1,0},{2,3},{3,2},{4,5},{5,4},{6,7},{7,6},{8,9},{9,8},{10,11... | collective-permute-start | bytes 6684680 | tf_op jit(solution)/shard_map/ppermute | solution.py:40
  73.0 4.0 %collective-permute-done.6.refs_2_ = bf16[128,2816]{1,0:T(8,128)(2,1)S(1)} collective-permute-done((bf16[128,2816]{1,0:T(8,128)(2,1)S(1)}, bf16[128,2816]{1,0:T(8,128)(2,1)S(1)}, u32[]{:S(2)}, u32[]{:S(2)}) %collective-permute-start.6) | collective-permute-done | bytes 720928 | tf_op jit(solution)/shard_map/ppermute | solution.py:322
  77.1 5.3 %collective-permute-start.7 = (bf16[128,2816]{1,0:T(8,128)(2,1)S(1)}, bf16[128,2816]{1,0:T(8,128)(2,1)S(1)}, u32[]{:S(2)}, u32[]{:S(2)}) collective-permute-start(bf16[128,2816]{1,0:T(8,128)(2,1)S(1)} %collective-permute-done.6.refs_2_), channel_id=1, source_target_pairs={{0,2},{1,15},{2,4},{3,1},{4,6},{5,3},{6,8},{7,5},{8,10},{9,7},{10,... | collective-permute-start | bytes 2162696 | tf_op jit(solution)/shard_map/ppermute | solution.py:322
  82.3 2.5 %collective-permute-done.3.refs_3_ = bf16[128,2816]{1,0:T(8,128)(2,1)S(1)} collective-permute-done((bf16[128,2816]{1,0:T(8,128)(2,1)S(1)}, bf16[128,2816]{1,0:T(8,128)(2,1)S(1)}, u32[]{:S(2)}, u32[]{:S(2)}) %collective-permute-start.3) | collective-permute-done | bytes 720928 | tf_op jit(solution)/shard_map/ppermute | solution.py:323
  84.8 5.3 %collective-permute-start.4 = (bf16[128,2816]{1,0:T(8,128)(2,1)S(1)}, bf16[128,2816]{1,0:T(8,128)(2,1)S(1)}, u32[]{:S(2)}, u32[]{:S(2)}) collective-permute-start(bf16[128,2816]{1,0:T(8,128)(2,1)S(1)} %collective-permute-done.3.refs_3_), channel_id=1, source_target_pairs={{0,2},{1,15},{2,4},{3,1},{4,6},{5,3},{6,8},{7,5},{8,10},{9,7},{10,... | collective-permute-start | bytes 2162696 | tf_op jit(solution)/shard_map/ppermute | solution.py:323
  90.0 2.5 %collective-permute-done.7.refs_4_ = bf16[128,2816]{1,0:T(8,128)(2,1)S(1)} collective-permute-done((bf16[128,2816]{1,0:T(8,128)(2,1)S(1)}, bf16[128,2816]{1,0:T(8,128)(2,1)S(1)}, u32[]{:S(2)}, u32[]{:S(2)}) %collective-permute-start.7) | collective-permute-done | bytes 720928 | tf_op jit(solution)/shard_map/ppermute | solution.py:322
  92.5 5.3 %collective-permute-start.8 = (bf16[128,2816]{1,0:T(8,128)(2,1)S(1)}, bf16[128,2816]{1,0:T(8,128)(2,1)S(1)}, u32[]{:S(2)}, u32[]{:S(2)}) collective-permute-start(bf16[128,2816]{1,0:T(8,128)(2,1)S(1)} %collective-permute-done.7.refs_4_), channel_id=1, source_target_pairs={{0,2},{1,15},{2,4},{3,1},{4,6},{5,3},{6,8},{7,5},{8,10},{9,7},{10,... | collective-permute-start | bytes 2162696 | tf_op jit(solution)/shard_map/ppermute | solution.py:322
  97.8 2.5 %collective-permute-done.4.refs_0_ = bf16[128,2816]{1,0:T(8,128)(2,1)S(1)} collective-permute-done((bf16[128,2816]{1,0:T(8,128)(2,1)S(1)}, bf16[128,2816]{1,0:T(8,128)(2,1)S(1)}, u32[]{:S(2)}, u32[]{:S(2)}) %collective-permute-start.4) | collective-permute-done | bytes 720928 | tf_op jit(solution)/shard_map/ppermute | solution.py:323
  100.2 5.4 %collective-permute-start.9 = (bf16[128,2816]{1,0:T(8,128)(2,1)S(1)}, bf16[128,2816]{1,0:T(8,128)(2,1)S(1)}, u32[]{:S(2)}, u32[]{:S(2)}) collective-permute-start(bf16[128,2816]{1,0:T(8,128)(2,1)S(1)} %collective-permute-done.4.refs_0_), channel_id=1, source_target_pairs={{0,2},{1,15},{2,4},{3,1},{4,6},{5,3},{6,8},{7,5},{8,10},{9,7},{10,... | collective-permute-start | bytes 2162696 | tf_op jit(solution)/shard_map/ppermute | solution.py:323
  105.6 2.3 %collective-permute-done.8.ref.refs_1_ = bf16[128,2816]{1,0:T(8,128)(2,1)S(1)} collective-permute-done((bf16[128,2816]{1,0:T(8,128)(2,1)S(1)}, bf16[128,2816]{1,0:T(8,128)(2,1)S(1)}, u32[]{:S(2)}, u32[]{:S(2)}) %collective-permute-start.8) | collective-permute-done | bytes 720928 | tf_op jit(solution)/shard_map/ppermute | solution.py:322
  108.0 5.0 %collective-permute-start.10 = (bf16[64,2816]{1,0:T(8,128)(2,1)S(1)}, bf16[64,2816]{1,0:T(8,128)(2,1)S(1)}, u32[]{:S(2)}, u32[]{:S(2)}) collective-permute-start(bf16[64,2816]{1,0:T(8,128)(2,1)S(1)} %head.2), channel_id=1, source_target_pairs={{0,2},{1,15},{2,4},{3,1},{4,6},{5,3},{6,8},{7,5},{8,10},{9,7},{10,... | collective-permute-start | bytes 1081352 | tf_op jit(solution)/shard_map/ppermute | solution.py:322
  113.0 2.7 %collective-permute-done.9.ref.refs_2_ = bf16[128,2816]{1,0:T(8,128)(2,1)S(1)} collective-permute-done((bf16[128,2816]{1,0:T(8,128)(2,1)S(1)}, bf16[128,2816]{1,0:T(8,128)(2,1)S(1)}, u32[]{:S(2)}, u32[]{:S(2)}) %collective-permute-start.9) | collective-permute-done | bytes 720928 | tf_op jit(solution)/shard_map/ppermute | solution.py:323
  115.7 5.0 %collective-permute-start.11 = (bf16[64,2816]{1,0:T(8,128)(2,1)S(1)}, bf16[64,2816]{1,0:T(8,128)(2,1)S(1)}, u32[]{:S(2)}, u32[]{:S(2)}) collective-permute-start(bf16[64,2816]{1,0:T(8,128)(2,1)S(1)} %head.3), channel_id=1, source_target_pairs={{0,2},{1,15},{2,4},{3,1},{4,6},{5,3},{6,8},{7,5},{8,10},{9,7},{10,... | collective-permute-start | bytes 1081352 | tf_op jit(solution)/shard_map/ppermute | solution.py:323
  120.8 3.7 %low_product.2 = (f32[2,64,512]{2,1,0:T(8,128)S(1)}, bf16[512,768]{1,0:T(8,128)(2,1)S(1)}) custom-call(s32[5]{0:T(128)S(1)} %stack.23.place, bf16[64,2816]{1,0:T(8,128)(2,1)} %get-tuple-element.12.refs_0_, bf16[64,2816]{1,0:T(8,128)(2,1)S(1)} %collective-permute-done.1.refs_0_.refs_1_, bf16[128,2816]{1,0:T(8,128)(2,1)S(1)} %collective-permute-done.6.refs_2_, ...), custom_call_target="tpu_custom_call" | custom-call | flops 2147483648 | bytes 2097152 | tf_op jit(solution)/shard_map/low_product/pallas_call | solution.py:247
  125.1 3.0 %low_product.3 = (bf16[8,64,128]{2,1,0:T(8,128)(2,1)S(1)}, bf16[512,768]{1,0:T(8,128)(2,1)S(1)}) custom-call(s32[5]{0:T(128)S(1)} %stack.23.place, bf16[128,2816]{1,0:T(8,128)(2,1)S(1)} %collective-permute-done.4.refs_0_, bf16[128,2816]{1,0:T(8,128)(2,1)S(1)} %collective-permute-done.8.ref.refs_1_, bf16[128,2816]{1,0:T(8,128)(2,1)S(1)} %collective-permute-done.9.ref.refs_2_, ...), custom_call_target="tpu_custom_call" | custom-call | flops 2147483648 | bytes 2097152 | tf_op jit(solution)/shard_map/low_product/pallas_call | solution.py:247
  129.0 1.6 %copy-done.3 = bf16[512,2176]{1,0:T(8,128)(2,1)S(1)} copy-done((bf16[512,2176]{1,0:T(8,128)(2,1)S(1)}, bf16[512,2176]{1,0:T(8,128)(2,1)}, u32[]{:S(2)}) %copy-start.3) | copy-done | bytes 2228248
  130.6 4.7 %base_product.1 = bf16[8,448,128]{2,1,0:T(8,128)(2,1)} custom-call(s32[5]{0:T(128)S(1)} %stack.23.place, bf16[384,2048]{1,0:T(8,128)(2,1)} %bitcast.6.base, bf16[512,2176]{1,0:T(8,128)(2,1)S(1)} %bitcast.16, bf16[512,2176]{1,0:T(8,128)(2,1)S(1)} %copy-done.3, bf16[8,64,128]{2,1,0:T(8,128)(2,1)S(1)} %get-tuple-element.14.low), custom_call_target="tpu_custom_call" | custom-call | flops 1610612736 | bytes 6029312 | tf_op jit(solution)/shard_map/base_product/pallas_call | solution.py:201
  135.3 6.2 %all-to-all-start.2 = ((bf16[8,448,128]{2,1,0:T(8,128)(2,1)}), bf16[8,448,128]{2,1,0:T(8,128)(2,1)S(1)}, u32[]{:S(2)}, u32[]{:S(2)}) async-start(bf16[8,448,128]{2,1,0:T(8,128)(2,1)} %base_product.1), calls=%async_computation.2 | async-start | bytes 1835008 | tf_op jit(solution)/shard_map/all_to_all | solution.py:44
  141.5 2.0 %collective-permute-start.13 = (bf16[512,768]{1,0:T(8,128)(2,1)}, bf16[512,768]{1,0:T(8,128)(2,1)S(1)}, u32[]{:S(2)}, u32[]{:S(2)}) collective-permute-start(bf16[512,768]{1,0:T(8,128)(2,1)} %copy-done.8), channel_id=1, source_target_pairs={{0,1},{1,0},{2,3},{3,2},{4,5},{5,4},{6,7},{7,6},{8,9},{9,8},{10,11... | collective-permute-start | bytes 2359304 | tf_op jit(solution)/shard_map/ppermute | solution.py:40
  143.5 2.3 %collective-permute-start.12 = (bf16[512,768]{1,0:T(8,128)(2,1)S(1)}, bf16[512,768]{1,0:T(8,128)(2,1)}, u32[]{:S(2)}, u32[]{:S(2)}) collective-permute-start(bf16[512,768]{1,0:T(8,128)(2,1)S(1)} %get-tuple-element.15.u_mine0), channel_id=1, source_target_pairs={{0,1},{1,0},{2,3},{3,2},{4,5},{5,4},{6,7},{7,6},{8,9},{9,8},{10,11... | collective-permute-start | bytes 2359304 | tf_op jit(solution)/shard_map/ppermute | solution.py:40
  145.9 2.0 %collective-permute-done.12.u_other0 = bf16[512,768]{1,0:T(8,128)(2,1)} collective-permute-done((bf16[512,768]{1,0:T(8,128)(2,1)S(1)}, bf16[512,768]{1,0:T(8,128)(2,1)}, u32[]{:S(2)}, u32[]{:S(2)}) %collective-permute-start.12) | collective-permute-done | bytes 786464 | tf_op jit(solution)/shard_map/ppermute | solution.py:40
  147.9 7.2 %all-to-all-done.2.got = bf16[8,448,128]{2,1,0:T(8,128)(2,1)S(1)} async-done(((bf16[8,448,128]{2,1,0:T(8,128)(2,1)}), bf16[8,448,128]{2,1,0:T(8,128)(2,1)S(1)}, u32[]{:S(2)}, u32[]{:S(2)}) %all-to-all-start.2) | async-done | bytes 917536 | tf_op jit(solution)/shard_map/all_to_all | solution.py:44
  156.1 4.2 %finish.1 = bf16[128,768]{1,0:T(8,128)(2,1)} custom-call(s32[5]{0:T(128)} %copy-done.11, bf16[8,448,128]{2,1,0:T(8,128)(2,1)} %copy-done.12, bf16[512,768]{1,0:T(8,128)(2,1)} %copy-done.7, bf16[512,768]{1,0:T(8,128)(2,1)} %copy-done.8, bf16[512,768]{1,0:T(8,128)(2,1)} %collective-permute-done.12.u_other0, bf16[512,768]{1,0:T(8,128)(2,1)} %copy-done.13, ...), custom_call_target="tpu_custom_call" | custom-call | flops 402653184 | bytes 917504 | tf_op jit(solution)/shard_map/finish/pallas_call | solution.py:293
  (45 shorter events, 10.6 us)
Async XLA Ops:
  0.8 1.6 copy-start.4
  2.4 1.8 %copy-start.10 = (bf16[8,128]{1,0:T(8,128)(2,1)}, bf16[8,128]{1,0:T(8,128)(2,1)S(1)}, u32[]{:S(2)}) copy-start(bf16[8,128]{1,0:T(8,128)(2,1)S(1)} %broadcast_in_dim.2.ids) | copy-start | bytes 6148
  2.8 1.4 copy-start
  4.2 5.1 %copy-start.5 = (bf16[1,8192,64]{1,2,0:T(8,128)(2,1)S(1)}, bf16[1,8192,64]{1,2,0:T(8,128)(2,1)}, u32[]{:S(2)}) copy-start(bf16[1,8192,64]{1,2,0:T(8,128)(2,1)} %param.8) | copy-start | bytes 3145732
  4.2 5.1 %copy-start.9 = (bf16[1,64,768]{2,1,0:T(8,128)(2,1)S(1)}, bf16[1,64,768]{2,1,0:T(8,128)(2,1)}, u32[]{:S(2)}) copy-start(bf16[1,64,768]{2,1,0:T(8,128)(2,1)} %param.9) | copy-start | bytes 294916
  4.2 46.0 %all-to-all-start.1 = ((bf16[4,128,2176]{2,1,0:T(8,128)(2,1)}), bf16[4,128,2176]{2,1,0:T(8,128)(2,1)S(1)}, u32[]{:S(2)}, u32[]{:S(2)}) async-start(bf16[4,128,2176]{2,1,0:T(8,128)(2,1)} %copy-done), calls=%async_computation.1 | async-start | bytes 4456448 | tf_op jit(solution)/shard_map/all_to_all | solution.py:44
  9.2 119.7 %copy-start.11 = (s32[5]{0:T(128)}, s32[5]{0:T(128)S(1)}, u32[]{:S(2)}) copy-start(s32[5]{0:T(128)S(1)} %stack.23.place) | copy-start | bytes 64
  10.6 28.2 %collective-permute-start.1 = (bf16[64,2816]{1,0:T(8,128)(2,1)S(1)}, bf16[64,2816]{1,0:T(8,128)(2,1)S(1)}, u32[]{:S(2)}, u32[]{:S(2)}) collective-permute-start(bf16[64,2816]{1,0:T(8,128)(2,1)S(1)} %get-tuple-element.11), channel_id=1, source_target_pairs={{0,272},{1,273},{2,274},{3,275},{4,276},{5,277},{6,278},{7,279},{8... | collective-permute-start | bytes 1081352 | tf_op jit(solution)/shard_map/ppermute | solution.py:316
  15.2 42.0 %collective-permute-start.5 = (bf16[64,2816]{1,0:T(8,128)(2,1)}, bf16[64,2816]{1,0:T(8,128)(2,1)S(1)}, u32[]{:S(2)}, u32[]{:S(2)}) collective-permute-start(bf16[64,2816]{1,0:T(8,128)(2,1)} %get-tuple-element.12.refs_0_), channel_id=1, source_target_pairs={{0,1},{1,0},{2,3},{3,2},{4,5},{5,4},{6,7},{7,6},{8,9},{9,8},{10,11... | collective-permute-start | bytes 1081352 | tf_op jit(solution)/shard_map/ppermute | solution.py:40
  38.8 30.0 %collective-permute-start.2 = (bf16[64,2816]{1,0:T(8,128)(2,1)S(1)}, bf16[64,2816]{1,0:T(8,128)(2,1)S(1)}, u32[]{:S(2)}, u32[]{:S(2)}) collective-permute-start(bf16[64,2816]{1,0:T(8,128)(2,1)S(1)} %collective-permute-done.1.refs_0_.refs_1_), channel_id=1, source_target_pairs={{0,1},{1,0},{2,3},{3,2},{4,5},{5,4},{6,7},{7,6},{8,9},{9,8},{10,11... | collective-permute-start | bytes 1081352 | tf_op jit(solution)/shard_map/ppermute | solution.py:40
  47.2 1.1 copy-start.6
  49.0 1.2 copy-start.1
  50.1 78.8 %all-to-all-start = ((bf16[16,24,2048]{2,1,0:T(8,128)(2,1)}), bf16[16,24,2048]{2,1,0:T(8,128)(2,1)}, u32[]{:S(2)}, u32[]{:S(2)}) async-start(bf16[16,24,2048]{2,1,0:T(8,128)(2,1)} %copy-done.1), calls=%async_computation | async-start | bytes 3145728 | tf_op jit(solution)/shard_map/all_to_all | solution.py:44
  58.2 18.9 %collective-permute-start.6 = (bf16[128,2816]{1,0:T(8,128)(2,1)S(1)}, bf16[128,2816]{1,0:T(8,128)(2,1)S(1)}, u32[]{:S(2)}, u32[]{:S(2)}) collective-permute-start(bf16[128,2816]{1,0:T(8,128)(2,1)S(1)} %join.3), channel_id=1, source_target_pairs={{0,2},{1,15},{2,4},{3,1},{4,6},{5,3},{6,8},{7,5},{8,10},{9,7},{10,... | collective-permute-start | bytes 2162696 | tf_op jit(solution)/shard_map/ppermute | solution.py:322
  68.9 15.9 %collective-permute-start.3 = (bf16[128,2816]{1,0:T(8,128)(2,1)S(1)}, bf16[128,2816]{1,0:T(8,128)(2,1)S(1)}, u32[]{:S(2)}, u32[]{:S(2)}) collective-permute-start(bf16[128,2816]{1,0:T(8,128)(2,1)S(1)} %join.2), channel_id=1, source_target_pairs={{0,2},{1,15},{2,4},{3,1},{4,6},{5,3},{6,8},{7,5},{8,10},{9,7},{10,... | collective-permute-start | bytes 2162696 | tf_op jit(solution)/shard_map/ppermute | solution.py:323
  71.1 49.6 %collective-permute-start = (bf16[512,2176]{1,0:T(8,128)(2,1)S(1)}, bf16[512,2176]{1,0:T(8,128)(2,1)S(1)}, u32[]{:S(2)}, u32[]{:S(2)}) collective-permute-start(bf16[512,2176]{1,0:T(8,128)(2,1)S(1)} %bitcast.13), channel_id=1, source_target_pairs={{0,1},{1,0},{2,3},{3,2},{4,5},{5,4},{6,7},{7,6},{8,9},{9,8},{10,11... | collective-permute-start | bytes 6684680 | tf_op jit(solution)/shard_map/ppermute | solution.py:40
  77.1 15.4 %collective-permute-start.7 = (bf16[128,2816]{1,0:T(8,128)(2,1)S(1)}, bf16[128,2816]{1,0:T(8,128)(2,1)S(1)}, u32[]{:S(2)}, u32[]{:S(2)}) collective-permute-start(bf16[128,2816]{1,0:T(8,128)(2,1)S(1)} %collective-permute-done.6.refs_2_), channel_id=1, source_target_pairs={{0,2},{1,15},{2,4},{3,1},{4,6},{5,3},{6,8},{7,5},{8,10},{9,7},{10,... | collective-permute-start | bytes 2162696 | tf_op jit(solution)/shard_map/ppermute | solution.py:322
  84.8 15.4 %collective-permute-start.4 = (bf16[128,2816]{1,0:T(8,128)(2,1)S(1)}, bf16[128,2816]{1,0:T(8,128)(2,1)S(1)}, u32[]{:S(2)}, u32[]{:S(2)}) collective-permute-start(bf16[128,2816]{1,0:T(8,128)(2,1)S(1)} %collective-permute-done.3.refs_3_), channel_id=1, source_target_pairs={{0,2},{1,15},{2,4},{3,1},{4,6},{5,3},{6,8},{7,5},{8,10},{9,7},{10,... | collective-permute-start | bytes 2162696 | tf_op jit(solution)/shard_map/ppermute | solution.py:323
  92.5 15.4 %collective-permute-start.8 = (bf16[128,2816]{1,0:T(8,128)(2,1)S(1)}, bf16[128,2816]{1,0:T(8,128)(2,1)S(1)}, u32[]{:S(2)}, u32[]{:S(2)}) collective-permute-start(bf16[128,2816]{1,0:T(8,128)(2,1)S(1)} %collective-permute-done.7.refs_4_), channel_id=1, source_target_pairs={{0,2},{1,15},{2,4},{3,1},{4,6},{5,3},{6,8},{7,5},{8,10},{9,7},{10,... | collective-permute-start | bytes 2162696 | tf_op jit(solution)/shard_map/ppermute | solution.py:322
  100.2 15.4 %collective-permute-start.9 = (bf16[128,2816]{1,0:T(8,128)(2,1)S(1)}, bf16[128,2816]{1,0:T(8,128)(2,1)S(1)}, u32[]{:S(2)}, u32[]{:S(2)}) collective-permute-start(bf16[128,2816]{1,0:T(8,128)(2,1)S(1)} %collective-permute-done.4.refs_0_), channel_id=1, source_target_pairs={{0,2},{1,15},{2,4},{3,1},{4,6},{5,3},{6,8},{7,5},{8,10},{9,7},{10,... | collective-permute-start | bytes 2162696 | tf_op jit(solution)/shard_map/ppermute | solution.py:323
  108.0 16.5 %collective-permute-start.10 = (bf16[64,2816]{1,0:T(8,128)(2,1)S(1)}, bf16[64,2816]{1,0:T(8,128)(2,1)S(1)}, u32[]{:S(2)}, u32[]{:S(2)}) collective-permute-start(bf16[64,2816]{1,0:T(8,128)(2,1)S(1)} %head.2), channel_id=1, source_target_pairs={{0,2},{1,15},{2,4},{3,1},{4,6},{5,3},{6,8},{7,5},{8,10},{9,7},{10,... | collective-permute-start | bytes 1081352 | tf_op jit(solution)/shard_map/ppermute | solution.py:322
  115.7 9.4 %collective-permute-start.11 = (bf16[64,2816]{1,0:T(8,128)(2,1)S(1)}, bf16[64,2816]{1,0:T(8,128)(2,1)S(1)}, u32[]{:S(2)}, u32[]{:S(2)}) collective-permute-start(bf16[64,2816]{1,0:T(8,128)(2,1)S(1)} %head.3), channel_id=1, source_target_pairs={{0,2},{1,15},{2,4},{3,1},{4,6},{5,3},{6,8},{7,5},{8,10},{9,7},{10,... | collective-permute-start | bytes 1081352 | tf_op jit(solution)/shard_map/ppermute | solution.py:323
  120.7 4.3 %copy-start.2 = (bf16[512,2176]{1,0:T(8,128)(2,1)}, bf16[512,2176]{1,0:T(8,128)(2,1)S(1)}, u32[]{:S(2)}) copy-start(bf16[512,2176]{1,0:T(8,128)(2,1)S(1)} %collective-permute-done.refs_6_.other) | copy-start | bytes 6684676
  124.4 19.1 %copy-start.7 = (bf16[512,768]{1,0:T(8,128)(2,1)}, bf16[512,768]{1,0:T(8,128)(2,1)S(1)}, u32[]{:S(2)}) copy-start(bf16[512,768]{1,0:T(8,128)(2,1)S(1)} %get-tuple-element.15.u_mine0) | copy-start | bytes 2359300
  128.1 0.9 copy-start.8
  129.0 1.6 %copy-start.3 = (bf16[512,2176]{1,0:T(8,128)(2,1)S(1)}, bf16[512,2176]{1,0:T(8,128)(2,1)}, u32[]{:S(2)}) copy-start(bf16[512,2176]{1,0:T(8,128)(2,1)} %copy-done.2) | copy-start | bytes 6684676
  135.3 19.8 %all-to-all-start.2 = ((bf16[8,448,128]{2,1,0:T(8,128)(2,1)}), bf16[8,448,128]{2,1,0:T(8,128)(2,1)S(1)}, u32[]{:S(2)}, u32[]{:S(2)}) async-start(bf16[8,448,128]{2,1,0:T(8,128)(2,1)} %base_product.1), calls=%async_computation.2 | async-start | bytes 1835008 | tf_op jit(solution)/shard_map/all_to_all | solution.py:44
  141.5 4.4 %collective-permute-start.13 = (bf16[512,768]{1,0:T(8,128)(2,1)}, bf16[512,768]{1,0:T(8,128)(2,1)S(1)}, u32[]{:S(2)}, u32[]{:S(2)}) collective-permute-start(bf16[512,768]{1,0:T(8,128)(2,1)} %copy-done.8), channel_id=1, source_target_pairs={{0,1},{1,0},{2,3},{3,2},{4,5},{5,4},{6,7},{7,6},{8,9},{9,8},{10,11... | collective-permute-start | bytes 2359304 | tf_op jit(solution)/shard_map/ppermute | solution.py:40
  143.5 4.3 %collective-permute-start.12 = (bf16[512,768]{1,0:T(8,128)(2,1)S(1)}, bf16[512,768]{1,0:T(8,128)(2,1)}, u32[]{:S(2)}, u32[]{:S(2)}) collective-permute-start(bf16[512,768]{1,0:T(8,128)(2,1)S(1)} %get-tuple-element.15.u_mine0), channel_id=1, source_target_pairs={{0,1},{1,0},{2,3},{3,2},{4,5},{5,4},{6,7},{7,6},{8,9},{9,8},{10,11... | collective-permute-start | bytes 2359304 | tf_op jit(solution)/shard_map/ppermute | solution.py:40
  145.9 9.2 %copy-start.13 = (bf16[512,768]{1,0:T(8,128)(2,1)}, bf16[512,768]{1,0:T(8,128)(2,1)S(1)}, u32[]{:S(2)}) copy-start(bf16[512,768]{1,0:T(8,128)(2,1)S(1)} %collective-permute-done.13.u_other1) | copy-start | bytes 2359300
  155.1 0.9 copy-start.12
